TPU v7x, 256 devices: a whole 4x4x8 slice. The times are simulated.
256 devices in a mesh: gx: 8 (over x_hi, y), gy: 32 (over z, x_lo, core).
Axes of the slice: x: 4 (x_hi: 2, x_lo: 2; x = x_hi * 2 + x_lo), y: 4, z: 8, core: 2. Of those that a mesh axis runs over, the one named last changes fastest.
Arguments:
- image: float32 [1024, 131072], P('gx', 'gy'), may hold values from -6 to 6
- psfs: bfloat16 [32, 64, 32, 1024], P('gx', 'gy'), may hold values from -0.11035156 to 0.11035156
Outputs:
- hessian_image: float32 [1024, 131072], P('gx', 'gy')
All inputs are finite; a program needn't handle non-finite values.
Results may differ from a plain program's by a relative error of at most 0.023.
Values may be sent and summed in bfloat16 or wider, within the bound.
A program may use at most 128 MiB of HBM per device.

v0:
```python
import math

import jax
import jax.numpy as jnp
from jax import lax
from jax.sharding import PartitionSpec as P

PATCH = 64
PSFW = 32
DEPTH = 64


BLEND = (0.125, 0.375, 0.375, 0.125)


def padded(cells, sides, width):
    for axis, dim in sides:
        count = lax.axis_size(axis)
        ends = count - 1
        head = lax.slice_in_dim(cells, 0, width, axis=dim)
        tail = lax.slice_in_dim(cells, cells.shape[dim] - width, cells.shape[dim], axis=dim)
        cells = jnp.concatenate(
            [
                lax.ppermute(tail, axis, [(i, (i + 1) % count) for i in range(ends)]),
                cells,
                lax.ppermute(head, axis, [((i + 1) % count, i) for i in range(ends)]),
            ],
            axis=dim,
        )
    return cells


def shortened(value):

    def short(part):
        return part.astype(jnp.bfloat16) if part.dtype == jnp.float32 else part

    return jax.tree.map(short, value)


def twiddle(rows, columns, offset, length):
    first = lax.broadcasted_iota(jnp.int32, (rows, columns), 0)
    second = lax.broadcasted_iota(jnp.int32, (rows, columns), 1) + offset
    phase = (first * second % length).astype(jnp.float32) * (2.0 * math.pi / length)
    return (jnp.cos(phase), jnp.sin(phase))


def trailing(table, data):
    return lax.dot_general(
        table, data, (((1,), (data.ndim - 1,)), ((), ())), preferred_element_type=jnp.float32
    )


def leading(data, table):
    return lax.dot_general(
        data, table, (((0,), (0,)), ((), ())), preferred_element_type=jnp.float32
    )


def forward(cube, length):
    count = cube.shape[-1]
    cosine, sine = twiddle(length, count, 0, length)
    cosine = cosine.astype(jnp.bfloat16)
    sine = sine.astype(jnp.bfloat16)
    real_part = trailing(cosine, cube).astype(jnp.bfloat16)
    imag_part = (-trailing(sine, cube)).astype(jnp.bfloat16)
    for _ in range(2):
        new_real = (trailing(cosine, real_part) + trailing(sine, imag_part)).astype(jnp.bfloat16)
        new_imag = (trailing(cosine, imag_part) - trailing(sine, real_part)).astype(jnp.bfloat16)
        real_part, imag_part = (new_real, new_imag)
    return (real_part, imag_part)


def multiply(left, right):
    left_re = left[0].astype(jnp.float32)
    left_im = left[1].astype(jnp.float32)
    right_re = right[0].astype(jnp.float32)
    right_im = right[1].astype(jnp.float32)
    real_part = left_re * right_re - left_im * right_im
    imag_part = left_re * right_im + left_im * right_re
    return (real_part.astype(jnp.bfloat16), imag_part.astype(jnp.bfloat16))


def inverse(spectrum, length):
    cosine, sine = twiddle(length, length, 0, length)
    cosine = cosine.astype(jnp.bfloat16)
    sine = sine.astype(jnp.bfloat16)
    scale = 1.0 / length
    real_part, imag_part = spectrum
    for _ in range(2):
        new_real = ((leading(real_part, cosine) - leading(imag_part, sine)) * scale).astype(
            jnp.bfloat16
        )
        new_imag = ((leading(imag_part, cosine) + leading(real_part, sine)) * scale).astype(
            jnp.bfloat16
        )
        real_part, imag_part = (new_real, new_imag)
    depth_cos, depth_sin = twiddle(length, DEPTH, PSFW // 2, length)
    result = (
        leading(real_part, depth_cos.astype(jnp.bfloat16))
        - leading(imag_part, depth_sin.astype(jnp.bfloat16))
    ) * scale
    return result.reshape(length, length * DEPTH)


def padded_along(values, axis, before, after):
    widths = [(0, 0)] * values.ndim
    widths[axis] = (before, after)
    return jnp.pad(values, widths)


def edge_bands(values, axis, width, inner):
    lower = lax.slice_in_dim(values, 0, width, axis=axis)
    upper = lax.slice_in_dim(values, width + inner, 2 * width + inner, axis=axis)
    return jnp.concatenate([lower, upper], axis)


def fold_bands(values, received, axis, width, inner):
    middle = lax.slice_in_dim(values, width, width + inner, axis=axis)
    total_len = received.shape[axis]
    lower = lax.slice_in_dim(received, 0, width, axis=axis)
    upper = lax.slice_in_dim(received, total_len - width, total_len, axis=axis)
    return (
        middle
        + padded_along(lower, axis, 0, inner - width)
        + padded_along(upper, axis, inner - width, 0)
    )


def body(image, psfs):
    patches = image.shape[0] // PATCH
    half = PSFW // 2
    tile = patches * PATCH
    length = PATCH + PSFW
    volume = PSFW * PSFW * PSFW
    weights = jnp.array(BLEND, jnp.float32)
    offset = lax.broadcasted_iota(
        jnp.int32, (patches, 2 * patches + 2), 1
    ) - 2 * lax.broadcasted_iota(jnp.int32, (patches, 2 * patches + 2), 0)
    across = jnp.zeros((patches, 2 * patches + 2), jnp.float32)
    for place in range(4):
        across = across + jnp.where(offset == place, weights[place], 0.0)
    cells = image.astype(jnp.bfloat16).reshape(patches, PATCH, PATCH, DEPTH)
    wider = padded(psfs, (("gx", 0), ("gy", 1)), 1)
    mixing = (
        (across[:, :, None] * weights[None, None, :])
        .reshape(patches, 4 * (2 * patches + 2))
        .astype(jnp.bfloat16)
    )
    blended = jnp.dot(
        mixing, wider.reshape(4 * (2 * patches + 2), volume), preferred_element_type=jnp.float32
    ).astype(jnp.bfloat16)
    blended = blended.reshape(patches, PSFW, PSFW, PSFW)

    def respond(pair):
        block, kernel = pair
        return inverse(multiply(forward(block, length), forward(kernel, length)), length)

    responses = lax.map(respond, (cells, blended))
    columns = length * DEPTH
    head = responses[:, :PATCH].reshape(tile, columns)
    tail = jnp.pad(responses[:, PATCH:], ((0, 0), (0, PATCH - PSFW), (0, 0))).reshape(tile, columns)
    extended = (
        jnp.pad(head, ((0, PSFW), (0, 0))) + jnp.pad(tail, ((PATCH, 0), (0, 0)))[: tile + PSFW]
    )
    band = half * DEPTH
    inner_cols = PATCH * DEPTH
    received = padded(
        edge_bands(extended, 0, half, tile).astype(jnp.bfloat16), (("gx", 0),), half
    ).astype(jnp.float32)
    merged = fold_bands(extended, received, 0, half, tile)
    received = padded(shortened(edge_bands(merged, 1, band, inner_cols)), (("gy", 1),), band)
    result = fold_bands(merged, received, 1, band, inner_cols)
    return result


def solution(mesh):
    placed = (P("gx", "gy"), P("gx", "gy", None, None))
    return jax.shard_map(body, mesh=mesh, in_specs=placed, out_specs=P("gx", "gy"), check_vma=False)
```

profile of v0, /device:TPU:123, one launch (start us, length us, event | category | flops | bytes accessed | tf_op | source)
XLA Modules:
  0.0 190.5 jit_solution(12563716969152113611)
XLA Ops:
  0.0 1.1 fusion.209
  1.1 3.4 %collective-permute-start = (bf16[1,2,32,1024]{3,2,1,0:T(8,128)(2,1)S(1)}, bf16[1,2,32,1024]{3,2,1,0:T(8,128)(2,1)S(1)}, u32[]{:S(2)}, u32[]{:S(2)}) collective-permute-start(bf16[1,2,32,1024]{3,2,1,0:T(8,128)(2,1)S(1)} %get-tuple-element.83), channel_id=1, source_target_pairs={{0,32},{32,64},{64,96},{96,128},{128,160},{160,192},{192,224},{1,3... | collective-permute-start | bytes 393224 | tf_op jit(solution)/shard_map/ppermute | solution.py:24
  4.6 1.9 %collective-permute-start.1 = (bf16[1,2,32,1024]{3,2,1,0:T(8,128)(2,1)S(1)}, bf16[1,2,32,1024]{3,2,1,0:T(8,128)(2,1)S(1)}, u32[]{:S(2)}, u32[]{:S(2)}) collective-permute-start(bf16[1,2,32,1024]{3,2,1,0:T(8,128)(2,1)S(1)} %get-tuple-element.82), channel_id=1, source_target_pairs={{32,0},{64,32},{96,64},{128,96},{160,128},{192,160},{224,192},{33,... | collective-permute-start | bytes 393224 | tf_op jit(solution)/shard_map/ppermute | solution.py:26
  8.5 5.4 %collective-permute-done.1 = bf16[1,2,32,1024]{3,2,1,0:T(8,128)(2,1)S(1)} collective-permute-done((bf16[1,2,32,1024]{3,2,1,0:T(8,128)(2,1)S(1)}, bf16[1,2,32,1024]{3,2,1,0:T(8,128)(2,1)S(1)}, u32[]{:S(2)}, u32[]{:S(2)}) %collective-permute-start.1) | collective-permute-done | bytes 131104 | tf_op jit(solution)/shard_map/ppermute | solution.py:26
  15.7 7.6 %collective-permute-start.2 = (bf16[6,1,32,1024]{3,2,1,0:T(8,128)(2,1)}, bf16[6,1,32,1024]{3,2,1,0:T(8,128)(2,1)S(1)}, u32[]{:S(2)}, u32[]{:S(2)}) collective-permute-start(bf16[6,1,32,1024]{3,2,1,0:T(8,128)(2,1)} %get-tuple-element.80), channel_id=1, source_target_pairs={{0,1},{1,2},{2,3},{3,4},{4,5},{5,6},{6,7},{7,8},{8,9},{9,10},{10,1... | collective-permute-start | bytes 1179656 | tf_op jit(solution)/shard_map/ppermute | solution.py:24
  23.3 1.9 %collective-permute-start.3 = (bf16[6,1,32,1024]{3,2,1,0:T(8,128)(2,1)}, bf16[6,1,32,1024]{3,2,1,0:T(8,128)(2,1)}, u32[]{:S(2)}, u32[]{:S(2)}) collective-permute-start(bf16[6,1,32,1024]{3,2,1,0:T(8,128)(2,1)} %get-tuple-element.81), channel_id=1, source_target_pairs={{1,0},{2,1},{3,2},{4,3},{5,4},{6,5},{7,6},{8,7},{9,8},{10,9},{11,1... | collective-permute-start | bytes 1179656 | tf_op jit(solution)/shard_map/ppermute | solution.py:26
  25.6 2.3 %reshape.79 = bf16[2,64,64,64]{3,2,1,0:T(8,128)(2,1)S(1)} reshape(bf16[128,4096]{1,0:T(8,128)(2,1)S(1)} %convert_element_type.343) | data formatting | bytes 2097152 | tf_op jit(solution)/shard_map/reshape | solution.py:143
  28.4 6.5 %collective-permute-done.3 = bf16[6,1,32,1024]{3,2,1,0:T(8,128)(2,1)} collective-permute-done((bf16[6,1,32,1024]{3,2,1,0:T(8,128)(2,1)}, bf16[6,1,32,1024]{3,2,1,0:T(8,128)(2,1)}, u32[]{:S(2)}, u32[]{:S(2)}) %collective-permute-start.3) | collective-permute-done | bytes 393248 | tf_op jit(solution)/shard_map/ppermute | solution.py:26
  34.9 1.4 pad_maximum_fusion
  37.9 105.7 %while.12 = (s32[]{:T(128)}, f32[2,96,6144]{1,2,0:T(8,128)}, bf16[2,64,64,64]{3,2,1,0:T(8,128)(2,1)S(1)}, bf16[2,32,32,32]{3,2,1,0:T(8,128)(2,1)S(1)}, s32[]{:T(128)}) while((s32[]{:T(128)}, f32[2,96,6144]{1,2,0:T(8,128)}, bf16[2,64,64,64]{3,2,1,0:T(8,128)(2,1)S(1)}, bf16[2,32,32,32]{3,2,1,0:T(8,128)(2,1)S(1)}, s32[]{:T(128)}) %tuple.36), condition=%wide.region_1.2_spmd, body=%wide.region_0.1_spmd.sunk | while | flops 2791944192 | bytes 191759440 | solution.py:159
  45.7 1.1 add_convert_fusion.8
  47.8 1.1 subtract_convert_fusion.11
  51.6 3.1 %fusion.368 = (bf16[96,96,96]{2,0,1:T(8,128)(2,1)S(1)}, bf16[96,96,96]{2,0,1:T(8,128)(2,1)S(1)}) fusion(bf16[96,96,96]{2,0,1:T(8,128)(2,1)S(1)} %add_convert_fusion.8, bf16[96,96,96]{2,0,1:T(8,128)(2,1)S(1)} %subtract_convert_fusion.10, bf16[96,96,96]{2,0,1:T(8,128)(2,1)S(1)} %subtract_convert_fusion.11, f32[96,96,96]{2,0,1:T(8,128)S(1)} %fusion.367, ...), kind=kOutput, calls=%fused_computation.5.clone.1 | convolution fusion | flops 69040128 | bytes 12976128 | tf_op jit(solution)/shard_map/while/body/eval_jaxpr/dot_general | solution.py:49
  56.9 2.6 %multiply_convert_fusion.9 = bf16[96,96,96]{2,1,0:T(8,128)(2,1)} fusion(f32[96,96,96]{2,1,0:T(8,128)S(1)} %fusion.369, bf16[96,96,96]{2,0,1:T(8,128)(2,1)S(1)} %get-tuple-element.112), kind=kOutput, calls=%fused_computation.10.clone.1 | convolution fusion | flops 172615680 | bytes 7077888 | tf_op jit(solution)/shard_map/while/body/eval_jaxpr/dot_general | solution.py:55
  59.5 3.9 %copy.90 = bf16[96,96,96]{0,2,1:T(8,128)(2,1)S(1)} copy(bf16[96,96,96]{2,1,0:T(8,128)(2,1)} %multiply_convert_fusion.9) | data formatting | bytes 3538944 | tf_op jit(solution)/shard_map/while/body/eval_jaxpr/convert_element_type | solution.py:94
  63.4 2.8 %fusion.371 = f32[96,96,96]{2,1,0:T(8,128)S(1)} fusion(bf16[96,96,96]{2,0,1:T(8,128)(2,1)} %copy-done), kind=kOutput, calls=%fused_computation.82.clone.1 | convolution fusion | flops 169961472 | bytes 5308416 | tf_op jit(solution)/shard_map/while/body/eval_jaxpr/dot_general | solution.py:55
  66.2 2.5 %multiply_convert_fusion.10 = bf16[96,96,96]{2,1,0:T(8,128)(2,1)} fusion(f32[96,96,96]{2,1,0:T(8,128)S(1)} %fusion.371, bf16[96,96,96]{2,0,1:T(8,128)(2,1)S(1)} %copy-done.3), kind=kOutput, calls=%fused_computation.11.clone.1 | convolution fusion | flops 172615680 | bytes 7077888 | tf_op jit(solution)/shard_map/while/body/eval_jaxpr/dot_general | solution.py:55
  68.7 5.0 %copy.91 = bf16[96,96,96]{0,2,1:T(8,128)(2,1)} copy(bf16[96,96,96]{2,1,0:T(8,128)(2,1)} %multiply_convert_fusion.10) | data formatting | bytes 3538944 | tf_op jit(solution)/shard_map/while/body/eval_jaxpr/convert_element_type | solution.py:91
  73.7 2.6 %fusion.373 = f32[96,96,96]{2,1,0:T(8,128)S(1)} fusion(bf16[96,96,96]{0,2,1:T(8,128)(2,1)} %copy.91), kind=kOutput, calls=%fused_computation.81.clone.1 | convolution fusion | flops 169961472 | bytes 5308416 | tf_op jit(solution)/shard_map/while/body/eval_jaxpr/dot_general | solution.py:55
  80.0 1.2 fusion.372
  81.2 1.6 subtract_multiply_fusion.2
  82.7 4.2 %copy.92 = f32[96,96,64]{0,2,1:T(8,128)} copy(f32[96,96,64]{1,2,0:T(8,128)S(1)} %subtract_multiply_fusion.2) | data formatting | bytes 4718592 | tf_op jit(solution)/shard_map/while/body/eval_jaxpr/mul | solution.py:99
  86.9 3.9 %constant_dynamic-update-slice_fusion.5 = f32[2,96,6144]{1,2,0:T(8,128)} fusion(f32[2,96,6144]{1,2,0:T(8,128)} %get-tuple-element.119, f32[1,96,6144]{1,2,0:T(8,128)} %bitcast.185, s32[]{:T(128)S(6)} %copy.98), kind=kLoop, calls=%fused_computation.133.clone.1 | loop fusion | bytes 6291460 | tf_op jit(solution)/shard_map/while/body/jit(dynamic_update_index_in_dim)/dynamic_update_slice | solution.py:159
  98.4 1.1 add_convert_fusion.8
  100.5 1.1 subtract_convert_fusion.11
  104.3 3.1 %fusion.368 = (bf16[96,96,96]{2,0,1:T(8,128)(2,1)S(1)}, bf16[96,96,96]{2,0,1:T(8,128)(2,1)S(1)}) fusion(bf16[96,96,96]{2,0,1:T(8,128)(2,1)S(1)} %add_convert_fusion.8, bf16[96,96,96]{2,0,1:T(8,128)(2,1)S(1)} %subtract_convert_fusion.10, bf16[96,96,96]{2,0,1:T(8,128)(2,1)S(1)} %subtract_convert_fusion.11, f32[96,96,96]{2,0,1:T(8,128)S(1)} %fusion.367, ...), kind=kOutput, calls=%fused_computation.5.clone.1 | convolution fusion | flops 69040128 | bytes 12976128 | tf_op jit(solution)/shard_map/while/body/eval_jaxpr/dot_general | solution.py:49
  109.6 2.6 %multiply_convert_fusion.9 = bf16[96,96,96]{2,1,0:T(8,128)(2,1)} fusion(f32[96,96,96]{2,1,0:T(8,128)S(1)} %fusion.369, bf16[96,96,96]{2,0,1:T(8,128)(2,1)S(1)} %get-tuple-element.112), kind=kOutput, calls=%fused_computation.10.clone.1 | convolution fusion | flops 172615680 | bytes 7077888 | tf_op jit(solution)/shard_map/while/body/eval_jaxpr/dot_general | solution.py:55
  112.2 3.9 %copy.90 = bf16[96,96,96]{0,2,1:T(8,128)(2,1)S(1)} copy(bf16[96,96,96]{2,1,0:T(8,128)(2,1)} %multiply_convert_fusion.9) | data formatting | bytes 3538944 | tf_op jit(solution)/shard_map/while/body/eval_jaxpr/convert_element_type | solution.py:94
  116.1 2.8 %fusion.371 = f32[96,96,96]{2,1,0:T(8,128)S(1)} fusion(bf16[96,96,96]{2,0,1:T(8,128)(2,1)} %copy-done), kind=kOutput, calls=%fused_computation.82.clone.1 | convolution fusion | flops 169961472 | bytes 5308416 | tf_op jit(solution)/shard_map/while/body/eval_jaxpr/dot_general | solution.py:55
  118.9 2.5 %multiply_convert_fusion.10 = bf16[96,96,96]{2,1,0:T(8,128)(2,1)} fusion(f32[96,96,96]{2,1,0:T(8,128)S(1)} %fusion.371, bf16[96,96,96]{2,0,1:T(8,128)(2,1)S(1)} %copy-done.3), kind=kOutput, calls=%fused_computation.11.clone.1 | convolution fusion | flops 172615680 | bytes 7077888 | tf_op jit(solution)/shard_map/while/body/eval_jaxpr/dot_general | solution.py:55
  121.4 5.0 %copy.91 = bf16[96,96,96]{0,2,1:T(8,128)(2,1)} copy(bf16[96,96,96]{2,1,0:T(8,128)(2,1)} %multiply_convert_fusion.10) | data formatting | bytes 3538944 | tf_op jit(solution)/shard_map/while/body/eval_jaxpr/convert_element_type | solution.py:91
  126.5 2.6 %fusion.373 = f32[96,96,96]{2,1,0:T(8,128)S(1)} fusion(bf16[96,96,96]{0,2,1:T(8,128)(2,1)} %copy.91), kind=kOutput, calls=%fused_computation.81.clone.1 | convolution fusion | flops 169961472 | bytes 5308416 | tf_op jit(solution)/shard_map/while/body/eval_jaxpr/dot_general | solution.py:55
  132.7 1.2 fusion.372
  133.9 1.6 subtract_multiply_fusion.2
  135.5 4.2 %copy.92 = f32[96,96,64]{0,2,1:T(8,128)} copy(f32[96,96,64]{1,2,0:T(8,128)S(1)} %subtract_multiply_fusion.2) | data formatting | bytes 4718592 | tf_op jit(solution)/shard_map/while/body/eval_jaxpr/mul | solution.py:99
  139.7 3.9 %constant_dynamic-update-slice_fusion.5 = f32[2,96,6144]{1,2,0:T(8,128)} fusion(f32[2,96,6144]{1,2,0:T(8,128)} %get-tuple-element.119, f32[1,96,6144]{1,2,0:T(8,128)} %bitcast.185, s32[]{:T(128)S(6)} %copy.98), kind=kLoop, calls=%fused_computation.133.clone.1 | loop fusion | bytes 6291460 | tf_op jit(solution)/shard_map/while/body/jit(dynamic_update_index_in_dim)/dynamic_update_slice | solution.py:159
  143.6 7.1 %slice.74 = f32[2,32,6144]{1,2,0:T(8,128)} slice(f32[2,96,6144]{1,2,0:T(8,128)} %get-tuple-element.59), slice={[0:2], [64:96], [0:6144]} | slice | bytes 3145728 | tf_op jit(solution)/shard_map/slice | solution.py:162
  150.6 4.4 %copy.33 = f32[2,64,6144]{2,1,0:T(8,128)S(1)} copy(f32[2,64,6144]{1,2,0:T(8,128)} %bitcast.186) | data formatting | bytes 6291456 | tf_op jit(solution)/shard_map/slice | solution.py:161
  155.0 5.5 %copy.41 = f32[2,32,6144]{2,1,0:T(8,128)} copy(f32[2,32,6144]{1,2,0:T(8,128)} %slice.74) | data formatting | bytes 3145728
  160.6 1.7 pad.29.clone
  162.9 1.9 %collective-permute-start.4 = (bf16[16,6144]{1,0:T(8,128)(2,1)S(1)}, bf16[16,6144]{1,0:T(8,128)(2,1)S(1)}, u32[]{:S(2)}, u32[]{:S(2)}) collective-permute-start(bf16[16,6144]{1,0:T(8,128)(2,1)S(1)} %get-tuple-element.74), channel_id=1, source_target_pairs={{0,32},{32,64},{64,96},{96,128},{128,160},{160,192},{192,224},{1,3... | collective-permute-start | bytes 589832 | tf_op jit(solution)/shard_map/ppermute | solution.py:24
  164.8 3.4 %collective-permute-start.5 = (bf16[16,6144]{1,0:T(8,128)(2,1)S(1)}, bf16[16,6144]{1,0:T(8,128)(2,1)S(1)}, u32[]{:S(2)}, u32[]{:S(2)}) collective-permute-start(bf16[16,6144]{1,0:T(8,128)(2,1)S(1)} %get-tuple-element.75), channel_id=1, source_target_pairs={{32,0},{64,32},{96,64},{128,96},{160,128},{192,160},{224,192},{33,... | collective-permute-start | bytes 589832 | tf_op jit(solution)/shard_map/ppermute | solution.py:26
  169.3 5.5 %collective-permute-done.5 = bf16[16,6144]{1,0:T(8,128)(2,1)S(1)} collective-permute-done((bf16[16,6144]{1,0:T(8,128)(2,1)S(1)}, bf16[16,6144]{1,0:T(8,128)(2,1)S(1)}, u32[]{:S(2)}, u32[]{:S(2)}) %collective-permute-start.5) | collective-permute-done | bytes 196640 | tf_op jit(solution)/shard_map/ppermute | solution.py:26
  175.4 3.7 %collective-permute-start.6 = (bf16[128,1024]{1,0:T(8,128)(2,1)S(1)}, bf16[128,1024]{1,0:T(8,128)(2,1)S(1)}, u32[]{:S(2)}, u32[]{:S(2)}) collective-permute-start(bf16[128,1024]{1,0:T(8,128)(2,1)S(1)} %get-tuple-element.76), channel_id=1, source_target_pairs={{0,1},{1,2},{2,3},{3,4},{4,5},{5,6},{6,7},{7,8},{8,9},{9,10},{10,1... | collective-permute-start | bytes 786440 | tf_op jit(solution)/shard_map/ppermute | solution.py:24
  179.2 1.9 %collective-permute-start.7 = (bf16[128,1024]{1,0:T(8,128)(2,1)S(1)}, bf16[128,1024]{1,0:T(8,128)(2,1)S(1)}, u32[]{:S(2)}, u32[]{:S(2)}) collective-permute-start(bf16[128,1024]{1,0:T(8,128)(2,1)S(1)} %get-tuple-element.77), channel_id=1, source_target_pairs={{1,0},{2,1},{3,2},{4,3},{5,4},{6,5},{7,6},{8,7},{9,8},{10,9},{11,1... | collective-permute-start | bytes 786440 | tf_op jit(solution)/shard_map/ppermute | solution.py:26
  181.1 1.4 collective-permute-done.6
  182.5 6.5 %collective-permute-done.7 = bf16[128,1024]{1,0:T(8,128)(2,1)S(1)} collective-permute-done((bf16[128,1024]{1,0:T(8,128)(2,1)S(1)}, bf16[128,1024]{1,0:T(8,128)(2,1)S(1)}, u32[]{:S(2)}, u32[]{:S(2)}) %collective-permute-start.7) | collective-permute-done | bytes 262176 | tf_op jit(solution)/shard_map/ppermute | solution.py:26
  189.0 1.5 fusion.197
  (103 shorter events, 42.4 us)
Async XLA Ops:
  0.0 25.3 %copy-start.10 = (f32[4]{0:T(128)S(1)}, f32[4]{0:T(128)}, u32[]{:S(2)}) copy-start(f32[4]{0:T(128)} %constant.85.clone) | copy-start | bytes 52
  0.0 25.5 %copy-start.9 = (f32[128,4096]{1,0:T(8,128)S(1)}, f32[128,4096]{1,0:T(8,128)}, u32[]{:S(2)}) copy-start(f32[128,4096]{1,0:T(8,128)} %param.5) | copy-start | bytes 6291460
  1.1 6.3 %collective-permute-start = (bf16[1,2,32,1024]{3,2,1,0:T(8,128)(2,1)S(1)}, bf16[1,2,32,1024]{3,2,1,0:T(8,128)(2,1)S(1)}, u32[]{:S(2)}, u32[]{:S(2)}) collective-permute-start(bf16[1,2,32,1024]{3,2,1,0:T(8,128)(2,1)S(1)} %get-tuple-element.83), channel_id=1, source_target_pairs={{0,32},{32,64},{64,96},{96,128},{128,160},{160,192},{192,224},{1,3... | collective-permute-start | bytes 393224 | tf_op jit(solution)/shard_map/ppermute | solution.py:24
  4.6 9.3 %collective-permute-start.1 = (bf16[1,2,32,1024]{3,2,1,0:T(8,128)(2,1)S(1)}, bf16[1,2,32,1024]{3,2,1,0:T(8,128)(2,1)S(1)}, u32[]{:S(2)}, u32[]{:S(2)}) collective-permute-start(bf16[1,2,32,1024]{3,2,1,0:T(8,128)(2,1)S(1)} %get-tuple-element.82), channel_id=1, source_target_pairs={{32,0},{64,32},{96,64},{128,96},{160,128},{192,160},{224,192},{33,... | collective-permute-start | bytes 393224 | tf_op jit(solution)/shard_map/ppermute | solution.py:26
  13.9 0.9 copy-start.8
  15.7 12.7 %collective-permute-start.2 = (bf16[6,1,32,1024]{3,2,1,0:T(8,128)(2,1)}, bf16[6,1,32,1024]{3,2,1,0:T(8,128)(2,1)S(1)}, u32[]{:S(2)}, u32[]{:S(2)}) collective-permute-start(bf16[6,1,32,1024]{3,2,1,0:T(8,128)(2,1)} %get-tuple-element.80), channel_id=1, source_target_pairs={{0,1},{1,2},{2,3},{3,4},{4,5},{5,6},{6,7},{7,8},{8,9},{9,10},{10,1... | collective-permute-start | bytes 1179656 | tf_op jit(solution)/shard_map/ppermute | solution.py:24
  23.3 11.5 %collective-permute-start.3 = (bf16[6,1,32,1024]{3,2,1,0:T(8,128)(2,1)}, bf16[6,1,32,1024]{3,2,1,0:T(8,128)(2,1)}, u32[]{:S(2)}, u32[]{:S(2)}) collective-permute-start(bf16[6,1,32,1024]{3,2,1,0:T(8,128)(2,1)} %get-tuple-element.81), channel_id=1, source_target_pairs={{1,0},{2,1},{3,2},{4,3},{5,4},{6,5},{7,6},{8,7},{9,8},{10,9},{11,1... | collective-permute-start | bytes 1179656 | tf_op jit(solution)/shard_map/ppermute | solution.py:26
  38.1 1.8 copy-start.4
  38.1 1.8 copy-start.6
  54.7 1.5 copy-start
  54.7 2.2 %copy-start.2 = (bf16[96,96,96]{2,0,1:T(8,128)(2,1)}, bf16[96,96,96]{2,0,1:T(8,128)(2,1)S(1)}, u32[]{:S(2)}) copy-start(bf16[96,96,96]{2,0,1:T(8,128)(2,1)S(1)} %get-tuple-element.111) | copy-start | bytes 5308420 | tf_op jit(solution)/shard_map/while
  63.4 2.8 %copy-start.3 = (bf16[96,96,96]{2,0,1:T(8,128)(2,1)S(1)}, bf16[96,96,96]{2,0,1:T(8,128)(2,1)}, u32[]{:S(2)}) copy-start(bf16[96,96,96]{2,0,1:T(8,128)(2,1)} %copy-done.2) | copy-start | bytes 5308420 | tf_op jit(solution)/shard_map/while
  77.3 1.7 copy-start.1
  86.9 3.9 %copy-start.5 = (bf16[2,64,64,64]{3,2,1,0:T(8,128)(2,1)S(1)}, bf16[2,64,64,64]{3,2,1,0:T(8,128)(2,1)}, u32[]{:S(2)}) copy-start(bf16[2,64,64,64]{3,2,1,0:T(8,128)(2,1)} %copy-done.4) | copy-start | bytes 3145732 | tf_op jit(solution)/shard_map/while
  86.9 3.9 %copy-start.7 = (bf16[2,32,32,32]{3,2,1,0:T(8,128)(2,1)S(1)}, bf16[2,32,32,32]{3,2,1,0:T(8,128)(2,1)}, u32[]{:S(2)}) copy-start(bf16[2,32,32,32]{3,2,1,0:T(8,128)(2,1)} %copy-done.6) | copy-start | bytes 393220 | tf_op jit(solution)/shard_map/while
  90.8 1.7 copy-start.4
  90.8 1.8 copy-start.6
  107.4 1.5 copy-start
  107.4 2.2 %copy-start.2 = (bf16[96,96,96]{2,0,1:T(8,128)(2,1)}, bf16[96,96,96]{2,0,1:T(8,128)(2,1)S(1)}, u32[]{:S(2)}) copy-start(bf16[96,96,96]{2,0,1:T(8,128)(2,1)S(1)} %get-tuple-element.111) | copy-start | bytes 5308420 | tf_op jit(solution)/shard_map/while
  116.1 2.8 %copy-start.3 = (bf16[96,96,96]{2,0,1:T(8,128)(2,1)S(1)}, bf16[96,96,96]{2,0,1:T(8,128)(2,1)}, u32[]{:S(2)}) copy-start(bf16[96,96,96]{2,0,1:T(8,128)(2,1)} %copy-done.2) | copy-start | bytes 5308420 | tf_op jit(solution)/shard_map/while
  130.0 1.7 copy-start.1
  139.7 3.9 %copy-start.5 = (bf16[2,64,64,64]{3,2,1,0:T(8,128)(2,1)S(1)}, bf16[2,64,64,64]{3,2,1,0:T(8,128)(2,1)}, u32[]{:S(2)}) copy-start(bf16[2,64,64,64]{3,2,1,0:T(8,128)(2,1)} %copy-done.4) | copy-start | bytes 3145732 | tf_op jit(solution)/shard_map/while
  139.7 3.9 %copy-start.7 = (bf16[2,32,32,32]{3,2,1,0:T(8,128)(2,1)S(1)}, bf16[2,32,32,32]{3,2,1,0:T(8,128)(2,1)}, u32[]{:S(2)}) copy-start(bf16[2,32,32,32]{3,2,1,0:T(8,128)(2,1)} %copy-done.6) | copy-start | bytes 393220 | tf_op jit(solution)/shard_map/while
  162.9 6.4 %collective-permute-start.4 = (bf16[16,6144]{1,0:T(8,128)(2,1)S(1)}, bf16[16,6144]{1,0:T(8,128)(2,1)S(1)}, u32[]{:S(2)}, u32[]{:S(2)}) collective-permute-start(bf16[16,6144]{1,0:T(8,128)(2,1)S(1)} %get-tuple-element.74), channel_id=1, source_target_pairs={{0,32},{32,64},{64,96},{96,128},{128,160},{160,192},{192,224},{1,3... | collective-permute-start | bytes 589832 | tf_op jit(solution)/shard_map/ppermute | solution.py:24
  164.8 10.0 %collective-permute-start.5 = (bf16[16,6144]{1,0:T(8,128)(2,1)S(1)}, bf16[16,6144]{1,0:T(8,128)(2,1)S(1)}, u32[]{:S(2)}, u32[]{:S(2)}) collective-permute-start(bf16[16,6144]{1,0:T(8,128)(2,1)S(1)} %get-tuple-element.75), channel_id=1, source_target_pairs={{32,0},{64,32},{96,64},{128,96},{160,128},{192,160},{224,192},{33,... | collective-permute-start | bytes 589832 | tf_op jit(solution)/shard_map/ppermute | solution.py:26
  175.4 7.0 %collective-permute-start.6 = (bf16[128,1024]{1,0:T(8,128)(2,1)S(1)}, bf16[128,1024]{1,0:T(8,128)(2,1)S(1)}, u32[]{:S(2)}, u32[]{:S(2)}) collective-permute-start(bf16[128,1024]{1,0:T(8,128)(2,1)S(1)} %get-tuple-element.76), channel_id=1, source_target_pairs={{0,1},{1,2},{2,3},{3,4},{4,5},{5,6},{6,7},{7,8},{8,9},{9,10},{10,1... | collective-permute-start | bytes 786440 | tf_op jit(solution)/shard_map/ppermute | solution.py:24
  179.2 9.8 %collective-permute-start.7 = (bf16[128,1024]{1,0:T(8,128)(2,1)S(1)}, bf16[128,1024]{1,0:T(8,128)(2,1)S(1)}, u32[]{:S(2)}, u32[]{:S(2)}) collective-permute-start(bf16[128,1024]{1,0:T(8,128)(2,1)S(1)} %get-tuple-element.77), channel_id=1, source_target_pairs={{1,0},{2,1},{3,2},{4,3},{5,4},{6,5},{7,6},{8,7},{9,8},{10,9},{11,1... | collective-permute-start | bytes 786440 | tf_op jit(solution)/shard_map/ppermute | solution.py:26
where the time goes:
time: 191 us; the launch traced here: 190 us
  matrix products  67.5 us (35%)
  local copies, waits for them, and re-layouts  64.3 us (34%)
  waiting for transfers between devices  27.7 us (15%)
  starting transfers between devices  25.8 us (14%)
  other arithmetic  4.36 us (2%)
    dot_general x20, matrix products, leading(): lax.dot_general(data, table, (((0,), (0,)), ((), ())), preferred_element_...  34.2 us
    dot_general x40, matrix products, trailing(): lax.dot_general(table, data, (((1,), (data.ndim - 1,)), ((), ())), prefer...  32.9 us
    ppermute x4, waiting for transfers between devices, padded(): lax.ppermute(head, axis, [((i + 1) % count, i) for i in range(ends)])  23.9 us
    ppermute x4, starting transfers between devices, padded(): lax.ppermute(tail, axis, [(i, (i + 1) % count) for i in range(ends)])  16.7 us
    convert_element_type x2, local copies, waits for them, and re-layouts, inverse(): ((leading(real_part, cosine) - leading(imag_part, sine)) * scale).astype(...  10 us
    ppermute x4, starting transfers between devices, padded(): lax.ppermute(head, axis, [((i + 1) % count, i) for i in range(ends)])  9.12 us
    mul x2, local copies, waits for them, and re-layouts, inverse(): (leading(real_part, depth_cos.astype(jnp.bfloat16)) - leading(imag_part,...  8.38 us
    unnamed x10, local copies, waits for them, and re-layouts  8.37 us
  transfers between devices with their start and end apart: 8, of which 8 were waited for; matrix products, arithmetic and copies ran while one was open for 2% of the time, Pallas kernels for 0%

commit v1 on v0

v1 whole, which is shorter than its diff:
```python
import math

import jax
import jax.numpy as jnp
import numpy as np
from jax import lax
from jax.experimental import pallas as pl
from jax.experimental.pallas import tpu as pltpu
from jax.sharding import PartitionSpec as P

PATCH = 64
PSFW = 32
DEPTH = 64
HALF = PSFW // 2
LXY = PATCH + PSFW
LZ = DEPTH + HALF
BINS = LXY // 2
PATCHES = 2
LANES = 128
TILE = PATCHES * PATCH
EXT = TILE + PSFW
SY = 2 * PATCH + 4
SP = 2 * PSFW + 4
SZ = 2 * LZ + 4
COLS = LXY * DEPTH
BLEND = (0.125, 0.375, 0.375, 0.125)
CORNER = BLEND[0] * BLEND[0]
PIECES = ((0, 1), (1, 1), (0, 1), (1, 1), (0, 1), (1, 1), (0, CORNER), (0, CORNER), (1, CORNER), (1, CORNER))
BAND = HALF * DEPTH
INNER = PATCH * DEPTH
MESH = pl.DeviceIdType.MESH
F32 = jnp.float32
BF16 = jnp.bfloat16


def tables():
    theta = 2.0 * math.pi * (np.arange(BINS) + 0.5) / LXY

    fx = np.zeros((2, LANES, PATCHES, PATCH))
    ang = theta[:, None] * np.arange(PATCH)[None, :]
    for p in range(PATCHES):
        fx[0, p * BINS:(p + 1) * BINS, p] = np.cos(ang)
        fx[1, p * BINS:(p + 1) * BINS, p] = -np.sin(ang)
    fx = fx.reshape(2 * LANES, TILE)

    ang = theta[:, None] * np.arange(PSFW)[None, :]
    bare = np.stack([np.cos(ang), -np.sin(ang)])
    own = np.zeros((2, LANES, 2 * PATCHES, 2, PSFW))
    for p in range(PATCHES):
        for a in range(4):
            row = 2 * p + a - 1
            if 0 <= row < 2 * PATCHES:
                for col in range(2):
                    own[:, p * BINS:(p + 1) * BINS, row, col] = BLEND[a] * BLEND[col + 1] * bare
    own = own.reshape(2 * LANES, -1)
    halo = np.zeros((2, LANES, len(PIECES), PSFW))
    for i, (p, weight) in enumerate(PIECES):
        halo[:, p * BINS:(p + 1) * BINS, i] = weight * bare
    halo = halo.reshape(2 * LANES, -1)

    def pair(cos, sin, sign):
        return np.stack([np.stack([cos, -sign * sin]), np.stack([sign * sin, cos])])

    def depth(count, depths):
        ang = 2.0 * math.pi / LZ * np.outer(np.arange(LZ), np.arange(depths))
        quad = pair(np.cos(ang), np.sin(ang), -1.0)
        out = np.zeros((2, count, LZ, 2, count, depths))
        for y in range(count):
            out[:, y, :, :, y, :] = quad.transpose(0, 2, 1, 3)
        return out.reshape(2 * count * LZ, 2 * count * depths)

    gz = depth(2, DEPTH)
    gzp = depth(4, PSFW)

    def flat(quad):
        o, i, r, c = quad.shape
        return quad.transpose(0, 2, 1, 3).reshape(o * r, i * c)

    ang = 2.0 * math.pi / LXY * np.outer(np.arange(LXY), np.arange(LXY))
    full = pair(np.cos(ang), np.sin(ang), -1.0)
    fy = flat(full[:, :, :, :PATCH])
    fyp = flat(full[:, :, :, :PSFW])
    gy = flat(pair(np.cos(ang), np.sin(ang), 1.0)) / LXY

    ang = 2.0 * math.pi / LZ * np.outer(np.arange(DEPTH) + HALF, np.arange(LZ))
    iz = flat(pair(np.cos(ang), np.sin(ang), 1.0)) / LZ

    ix = np.zeros((EXT, 2, LANES))
    ang = np.arange(LXY)[:, None] * theta[None, :]
    for p in range(PATCHES):
        ix[p * PATCH:p * PATCH + LXY, 0, p * BINS:(p + 1) * BINS] = np.cos(ang) * 2.0 / LXY
        ix[p * PATCH:p * PATCH + LXY, 1, p * BINS:(p + 1) * BINS] = -np.sin(ang) * 2.0 / LXY
    ix = ix.reshape(EXT, 2 * LANES)

    return [jnp.asarray(t, BF16) for t in [fx, gz, gzp, fy, fyp, gy, iz, ix, own, halo]]


def mm(a, b):
    return lax.dot_general(a, b, (((1,), (0,)), ((), ())), preferred_element_type=F32)


def mm_t(a, b):
    return lax.dot_general(a, b, (((1,), (1,)), ((), ())), preferred_element_type=F32)


SIDES = ((0, -1), (0, 1), (-1, 0), (1, 0), (-1, -1), (-1, 1), (1, -1), (1, 1))
LEFT, RIGHT, UP, DOWN, UL, UR, DL, DR = range(8)
BACK = (RIGHT, LEFT, DOWN, UP, DR, DL, UR, UL)
HALO = ((0, 64), (64, 64), (128, 32), (160, 32), (192, 32), (224, 32), (256, 32), (288, 32))
NODE = PSFW
GROUPS = LXY // 4
U_DEPTH, U_IMAGE, U_PSF, U_BACK, U_INNER = 4, 4, 2, 4, 4
EDGE = HALF // 4


def kernel(image, psfs, fx, gz, gzp, fy, fyp, gy, iz, ix, pown, phalo,
           result,
           img, own, part, halo, d1, e1, spec, pspec, ispec, resp, out,
           ysend, xsend, yrecv, xrecv, crecv,
           image_sem, own_sem, out_sem, psend_sem, precv_sem, rsend_sem, rrecv_sem):
    gx, gy_ = lax.axis_index("gx"), lax.axis_index("gy")
    last_x, last_y = lax.axis_size("gx") - 1, lax.axis_size("gy") - 1

    def present(side):
        dx, dy = SIDES[side]
        terms = []
        if dx:
            terms.append(gx > 0 if dx < 0 else gx < last_x)
        if dy:
            terms.append(gy_ > 0 if dy < 0 else gy_ < last_y)
        return terms[0] if len(terms) == 1 else jnp.logical_and(terms[0], terms[1])

    def place(side):
        dx, dy = SIDES[side]
        return (gx + dx, gy_ + dy)

    own_copy = pltpu.make_async_copy(psfs, own, own_sem)
    own_copy.start()
    chunk = INNER // 4
    image_copies = []
    for t in range(4):
        sl = pl.ds(t * chunk, chunk)
        image_copies.append(pltpu.make_async_copy(image.at[:, sl], img.at[:, sl], image_sem.at[t]))
        image_copies[-1].start()

    barrier = pltpu.get_barrier_semaphore()
    count = jnp.int32(0)
    for side in range(8):
        count = count + present(side).astype(jnp.int32)

        @pl.when(present(side))
        def _():
            pl.semaphore_signal(barrier, inc=1, device_id=place(side), device_id_type=MESH)

    own_copy.wait()

    def node(r, c):
        row = (r * 2 + c) * NODE
        return own[row:row + NODE, :].astype(F32)

    def put(row, value):
        part[row:row + NODE, :] = value.astype(BF16)

    w0, w1 = BLEND[0], BLEND[1]
    for col, at in ((0, 0), (1, 64)):
        n0, n1, n2, n3 = (node(r, col) for r in range(4))
        put(at, (w0 * w1) * (n0 + n1) + (w0 * w0) * n2)
        put(at + NODE, (w0 * w0) * n1 + (w0 * w1) * (n2 + n3))
    put(128, (w0 * w1) * (node(0, 0) + node(0, 1)))
    put(160, (w0 * w1) * (node(3, 0) + node(3, 1)))
    corner = {UL: 0, UR: 1, DL: 6, DR: 7}

    def psf_copy(side, target=None):
        if side in corner:
            src = own.at[pl.ds(corner[side] * NODE, NODE), :]
        else:
            src = part.at[pl.ds(*HALO[side]), :]
        return pltpu.make_async_remote_copy(
            src_ref=src, dst_ref=halo.at[pl.ds(*HALO[BACK[side]]), :],
            send_sem=psend_sem.at[side], recv_sem=precv_sem.at[BACK[side]],
            device_id=place(side if target is None else target), device_id_type=MESH)

    pl.semaphore_wait(barrier, count)
    for side in range(8):
        @pl.when(present(side))
        def _():
            psf_copy(side).start()

        @pl.when(jnp.logical_not(present(side)))
        def _():
            halo[pl.ds(*HALO[side]), :] = jnp.zeros((HALO[side][1], PSFW * PSFW), BF16)

    width = 512
    for t in range(INNER // width):
        if t % (chunk // width) == 0:
            image_copies[t // (chunk // width)].wait()
        sl = slice(t * width, (t + 1) * width)
        d1[:, sl] = mm(fx[...], img[:, sl].astype(BF16)).astype(BF16)

    def depth_step(ref, table, t, ylo, width_y, stride, out):
        def rhs(tile):
            sl = pl.ds(pl.multiple_of(tile * LANES, LANES), LANES)
            return jnp.concatenate([ref[:LANES, sl], ref[LANES:, sl]], axis=1)

        both = jnp.concatenate([rhs(2 * t), rhs(2 * t + 1)], axis=0)
        res = mm_t(table[...], both)
        for jj in range(2):
            for part in range(2):
                for y in range(ylo):
                    row = (part * ylo + y) * LZ
                    block = res[row:row + LZ, jj * LANES:(jj + 1) * LANES]
                    start = part * width_y + (2 * t + jj) * ylo + y
                    out[pl.ds(start, LZ, stride=stride), :] = block

    @pl.loop(0, 16, unroll=U_DEPTH)
    def _(t):
        depth_step(d1, gz, t, 2, PATCH, SY, spec)

    def slab(ref, t, rows, stride):
        parts = [ref[pl.ds((2 * t + h) * stride, rows), :] for h in range(2)]
        return jnp.concatenate(parts, axis=1).astype(BF16)

    @pl.loop(0, LZ // 2, unroll=U_IMAGE)
    def _(t):
        ispec[t] = mm(fy[...], slab(spec, t, 2 * PATCH, SY)).astype(BF16)

    for side in range(8):
        @pl.when(present(side))
        def _():
            psf_copy(BACK[side], side).wait_recv()
    for t in range(2):
        sl = slice(t * 512, (t + 1) * 512)
        e1[:, sl] = (mm(pown[...], own[:, sl]) + mm(phalo[...], halo[:, sl])).astype(BF16)

    @pl.loop(0, 4, unroll=U_PSF)
    def _(t):
        depth_step(e1, gzp, t, 4, PSFW, SP, pspec)

    @pl.loop(0, LZ // 2, unroll=U_BACK)
    def _(t):
        b = mm(fyp[...], slab(pspec, t, 2 * PSFW, SP))
        a = ispec[t].astype(F32)
        ar, ai, br, bi = a[:LXY], a[LXY:], b[:LXY], b[LXY:]
        prod = jnp.concatenate([ar * br - ai * bi, ar * bi + ai * br], axis=0).astype(BF16)
        back = mm(gy[...], prod)
        for h in range(2):
            for part_ in range(2):
                block = back[part_ * LXY:(part_ + 1) * LXY, h * LANES:(h + 1) * LANES]
                resp[pl.ds(part_ * LZ + 2 * t + h, LXY, stride=SZ), :] = block

    def group(g):
        rows = []
        for h in range(2):
            parts = [resp[pl.ds((4 * g + 2 * h + q) * SZ, 2 * LZ), :] for q in range(2)]
            flat = jnp.concatenate(parts, axis=1).astype(BF16)
            z = mm(iz[...], flat).astype(BF16)
            for q in range(2):
                half = z[:, q * LANES:(q + 1) * LANES]
                rows.append(jnp.concatenate([half[:DEPTH], half[DEPTH:]], axis=1))
        return mm_t(ix[...], jnp.concatenate(rows, axis=0))

    for side in range(2):
        @pl.loop(0, EDGE, unroll=EDGE)
        def _(e):
            cols = pl.ds(pl.multiple_of(e * 256, 256), 256)
            ysend[side, :, cols] = group(e + side * (GROUPS - EDGE)).astype(BF16)

    def y_copy(side, target):
        dx, dy = SIDES[side]
        rows = {0: pl.ds(HALF, TILE), -1: pl.ds(0, HALF), 1: pl.ds(HALF + TILE, HALF)}[dx]
        dst = yrecv.at[BACK[side]] if dx == 0 else crecv.at[BACK[side] - 4]
        return pltpu.make_async_remote_copy(
            src_ref=ysend.at[side if dx == 0 else (dy + 1) // 2, rows, :], dst_ref=dst,
            send_sem=rsend_sem.at[side], recv_sem=rrecv_sem.at[BACK[side]],
            device_id=place(side if target is None else target), device_id_type=MESH)

    def x_copy(side, target):
        return pltpu.make_async_remote_copy(
            src_ref=xsend.at[side - 2], dst_ref=xrecv.at[BACK[side] - 2],
            send_sem=rsend_sem.at[side], recv_sem=rrecv_sem.at[BACK[side]],
            device_id=place(side if target is None else target), device_id_type=MESH)

    def response_copy(side, target=None):
        return (x_copy if side in (UP, DOWN) else y_copy)(side, target)

    for side in (LEFT, RIGHT, UL, UR, DL, DR):
        @pl.when(present(side))
        def _():
            response_copy(side).start()

    @pl.loop(0, GROUPS - 2 * EDGE, unroll=U_INNER)
    def _(g):
        cols = pl.ds(pl.multiple_of(g * 256, 256), 256)
        value = group(g + EDGE)
        out[:, cols] = value[HALF:HALF + TILE]
        xsend[0, :, cols] = value[:HALF].astype(BF16)
        xsend[1, :, cols] = value[HALF + TILE:].astype(BF16)

    for side in (UP, DOWN):
        @pl.when(present(side))
        def _():
            response_copy(side).start()

    def arrive(side, rows, cols, ref):
        @pl.when(present(side))
        def _():
            response_copy(BACK[side], side).wait_recv()
            out[rows, cols] += ref[...].astype(F32)

    top, bottom = pl.ds(0, HALF), pl.ds(TILE - HALF, HALF)
    first, last = pl.ds(0, BAND), pl.ds(INNER - BAND, BAND)
    every = pl.ds(0, TILE)
    arrive(UP, top, pl.ds(0, INNER), xrecv.at[0])
    arrive(DOWN, bottom, pl.ds(0, INNER), xrecv.at[1])
    middle = pltpu.make_async_copy(
        out.at[:, pl.ds(BAND, INNER - 2 * BAND)], result.at[:, pl.ds(BAND, INNER - 2 * BAND)], out_sem.at[0])
    middle.start()
    arrive(UL, top, first, crecv.at[0])
    arrive(DL, bottom, first, crecv.at[2])
    arrive(LEFT, every, first, yrecv.at[0])
    one = pltpu.make_async_copy(out.at[:, first], result.at[:, first], out_sem.at[1])
    one.start()
    arrive(UR, top, last, crecv.at[1])
    arrive(DR, bottom, last, crecv.at[3])
    arrive(RIGHT, every, last, yrecv.at[1])
    two = pltpu.make_async_copy(out.at[:, last], result.at[:, last], out_sem.at[2])
    two.start()

    for side in range(8):
        @pl.when(present(side))
        def _():
            psf_copy(side).wait_send()
            response_copy(side).wait_send()
    middle.wait()
    one.wait()
    two.wait()


def compute(image, psfs, *consts):
    vmem, anywhere = pl.BlockSpec(memory_space=pltpu.VMEM), pl.BlockSpec(memory_space=pl.ANY)
    dma = pltpu.SemaphoreType.DMA
    return pl.pallas_call(
        kernel,
        out_shape=jax.ShapeDtypeStruct((TILE, INNER), F32),
        in_specs=[anywhere, anywhere] + [vmem] * len(consts),
        out_specs=anywhere,
        scratch_shapes=[
            pltpu.VMEM((TILE, INNER), F32),
            pltpu.VMEM((8 * PSFW, PSFW * PSFW), BF16),
            pltpu.VMEM((6 * PSFW, PSFW * PSFW), BF16),
            pltpu.VMEM((10 * PSFW, PSFW * PSFW), BF16),
            pltpu.VMEM((2 * LANES, INNER), BF16),
            pltpu.VMEM((2 * LANES, PSFW * PSFW), BF16),
            pltpu.VMEM((LZ * SY, LANES), F32),
            pltpu.VMEM((LZ * SP, LANES), F32),
            pltpu.VMEM((LZ // 2, 2 * LXY, 2 * LANES), BF16),
            pltpu.VMEM((LXY * SZ, LANES), F32),
            pltpu.VMEM((TILE, INNER), F32),
            pltpu.VMEM((2, EXT, BAND), BF16),
            pltpu.VMEM((2, HALF, INNER), BF16),
            pltpu.VMEM((2, TILE, BAND), BF16),
            pltpu.VMEM((2, HALF, INNER), BF16),
            pltpu.VMEM((4, HALF, BAND), BF16),
            dma((4,)), dma, dma((3,)), dma((8,)), dma((8,)), dma((8,)), dma((8,)),
        ],
        compiler_params=pltpu.CompilerParams(
            vmem_limit_bytes=60 * 1024 * 1024, collective_id=0, has_side_effects=True),
    )(image, psfs.reshape(8 * PSFW, PSFW * PSFW), *consts)


def body(image, psfs):
    return compute(image, psfs, *tables())


def solution(mesh):
    placed = (P("gx", "gy"), P("gx", "gy", None, None))
    return jax.shard_map(body, mesh=mesh, in_specs=placed, out_specs=P("gx", "gy"), check_vma=False)
```

time: 191 us -> 42.6 us (0.22)
  the two profiles are of different devices: /device:TPU:123 before, /device:TPU:166 now
where the time goes in v1:
time: 42.6 us; the launch traced here: 42.4 us
  Pallas kernels  39.3 us (92%)
  local copies, waits for them, and re-layouts  3.11 us (7%)
    pallas_call x1, Pallas kernels, compute(): pl.pallas_call(kernel, out_shape=jax.ShapeDtypeStruct((TILE, INNER), F32)...  39.3 us
    unnamed x1, local copies, waits for them, and re-layouts  3.11 us

profile of v1, /device:TPU:166, one launch (start us, length us, event | category | flops | bytes accessed | tf_op | source)
XLA Modules:
  0.0 42.4 jit_solution(2391737550186086092)
XLA Ops:
  0.0 39.3 %shard_map.118 = f32[128,4096]{1,0:T(8,128)} custom-call(f32[128,4096]{1,0:T(8,128)} %image.1, bf16[256,1024]{1,0:T(8,128)(2,1)} %bitcast.1, bf16[256,128]{1,0:T(8,128)(2,1)} %constant.20.clone.fx, bf16[320,256]{1,0:T(8,128)(2,1)} %constant.21.clone.gz, bf16[640,256]{1,0:T(8,128)(2,1)} %constant.22.clone.gzp, bf16[192,128]{1,0:T(8,128)(2,1)} %constant.23.clone.fy, ...), custom_call_target="tpu_custom_call" | custom-call | tf_op jit(solution)/shard_map/pallas_call | solution.py:342
  39.3 3.1 %copy.14 = f32[128,4096]{1,0:T(8,128)} copy(f32[128,4096]{1,0:T(8,128)} %shard_map.118) | data formatting | bytes 4194304

commit v2 on v1

--- a/solution.py
+++ b/solution.py
@@ -109,15 +109,15 @@
 HALO = ((0, 64), (64, 64), (128, 32), (160, 32), (192, 32), (224, 32), (256, 32), (288, 32))
 NODE = PSFW
 GROUPS = LXY // 4
-U_DEPTH, U_IMAGE, U_PSF, U_BACK, U_INNER = 4, 4, 2, 4, 4
+U_DEPTH, U_IMAGE, U_PSF, U_BACK, U_INNER = 16, 40, 4, 40, 16
 EDGE = HALF // 4
 
 
 def kernel(image, psfs, fx, gz, gzp, fy, fyp, gy, iz, ix, pown, phalo,
-           result,
-           img, own, part, halo, d1, e1, spec, pspec, ispec, resp, out,
+           out,
+           img, own, part, halo, d1, e1, spec, pspec, ispec, resp,
            ysend, xsend, yrecv, xrecv, crecv,
-           image_sem, own_sem, out_sem, psend_sem, precv_sem, rsend_sem, rrecv_sem):
+           image_sem, own_sem, psend_sem, precv_sem, rsend_sem, rrecv_sem):
     gx, gy_ = lax.axis_index("gx"), lax.axis_index("gy")
     last_x, last_y = lax.axis_size("gx") - 1, lax.axis_size("gy") - 1
 
@@ -238,10 +238,10 @@
 
     @pl.loop(0, LZ // 2, unroll=U_BACK)
     def _(t):
-        b = mm(fyp[...], slab(pspec, t, 2 * PSFW, SP))
-        a = ispec[t].astype(F32)
+        b = mm(fyp[...], slab(pspec, t, 2 * PSFW, SP)).astype(BF16)
+        a = ispec[t]
         ar, ai, br, bi = a[:LXY], a[LXY:], b[:LXY], b[LXY:]
-        prod = jnp.concatenate([ar * br - ai * bi, ar * bi + ai * br], axis=0).astype(BF16)
+        prod = jnp.concatenate([ar * br - ai * bi, ar * bi + ai * br], axis=0)
         back = mm(gy[...], prod)
         for h in range(2):
             for part_ in range(2):
@@ -312,38 +312,27 @@
     every = pl.ds(0, TILE)
     arrive(UP, top, pl.ds(0, INNER), xrecv.at[0])
     arrive(DOWN, bottom, pl.ds(0, INNER), xrecv.at[1])
-    middle = pltpu.make_async_copy(
-        out.at[:, pl.ds(BAND, INNER - 2 * BAND)], result.at[:, pl.ds(BAND, INNER - 2 * BAND)], out_sem.at[0])
-    middle.start()
     arrive(UL, top, first, crecv.at[0])
     arrive(DL, bottom, first, crecv.at[2])
     arrive(LEFT, every, first, yrecv.at[0])
-    one = pltpu.make_async_copy(out.at[:, first], result.at[:, first], out_sem.at[1])
-    one.start()
     arrive(UR, top, last, crecv.at[1])
     arrive(DR, bottom, last, crecv.at[3])
     arrive(RIGHT, every, last, yrecv.at[1])
-    two = pltpu.make_async_copy(out.at[:, last], result.at[:, last], out_sem.at[2])
-    two.start()
-
     for side in range(8):
         @pl.when(present(side))
         def _():
             psf_copy(side).wait_send()
             response_copy(side).wait_send()
-    middle.wait()
-    one.wait()
-    two.wait()
 
 
 def compute(image, psfs, *consts):
-    vmem, anywhere = pl.BlockSpec(memory_space=pltpu.VMEM), pl.BlockSpec(memory_space=pl.ANY)
+    vmem, anywhere = pl.BlockSpec(memory_space=pltpu.VMEM), pl.BlockSpec(memory_space=pltpu.HBM)
     dma = pltpu.SemaphoreType.DMA
     return pl.pallas_call(
         kernel,
         out_shape=jax.ShapeDtypeStruct((TILE, INNER), F32),
         in_specs=[anywhere, anywhere] + [vmem] * len(consts),
-        out_specs=anywhere,
+        out_specs=vmem,
         scratch_shapes=[
             pltpu.VMEM((TILE, INNER), F32),
             pltpu.VMEM((8 * PSFW, PSFW * PSFW), BF16),
@@ -355,16 +344,15 @@
             pltpu.VMEM((LZ * SP, LANES), F32),
             pltpu.VMEM((LZ // 2, 2 * LXY, 2 * LANES), BF16),
             pltpu.VMEM((LXY * SZ, LANES), F32),
-            pltpu.VMEM((TILE, INNER), F32),
             pltpu.VMEM((2, EXT, BAND), BF16),
             pltpu.VMEM((2, HALF, INNER), BF16),
             pltpu.VMEM((2, TILE, BAND), BF16),
             pltpu.VMEM((2, HALF, INNER), BF16),
             pltpu.VMEM((4, HALF, BAND), BF16),
-            dma((4,)), dma, dma((3,)), dma((8,)), dma((8,)), dma((8,)), dma((8,)),
+            dma((4,)), dma, dma((8,)), dma((8,)), dma((8,)), dma((8,)),
         ],
         compiler_params=pltpu.CompilerParams(
-            vmem_limit_bytes=60 * 1024 * 1024, collective_id=0, has_side_effects=True),
+            vmem_limit_bytes=49 * 1024 * 1024, collective_id=0, has_side_effects=True),
     )(image, psfs.reshape(8 * PSFW, PSFW * PSFW), *consts)
 
 

time: 42.6 us -> 43.8 us (1.028)
  local copies, waits for them, and re-layouts: 3.11 us -> 11.1 us
  Pallas kernels: 39.3 us -> 32.1 us
    unnamed x1 -> x23, local copies, waits for them, and re-layouts: 3.11 us -> 11.1 us
    pallas_call x1, Pallas kernels: 39.3 us -> 32.1 us  [compute(): pl.pallas_call(kernel, out_shape=jax.ShapeDtypeStruct((TILE, INNER), F32)...]
where the time goes in v2:
time: 43.8 us; the launch traced here: 43.3 us
  Pallas kernels  32.1 us (73%)
  local copies, waits for them, and re-layouts  11.1 us (25%)
    pallas_call x1, Pallas kernels, compute(): pl.pallas_call(kernel, out_shape=jax.ShapeDtypeStruct((TILE, INNER), F32)...  32.1 us
    unnamed x23, local copies, waits for them, and re-layouts  11.1 us

profile of v2, /device:TPU:166, one launch (start us, length us, event | category | flops | bytes accessed | tf_op | source)
XLA Modules:
  0.0 43.3 jit_solution(6899373930430127746)
XLA Ops:
  0.0 0.0 copy-start
  0.0 1.0 %copy-done = bf16[4,2,32,1024]{3,2,1,0:T(8,128)(2,1)S(1)} copy-done((bf16[4,2,32,1024]{3,2,1,0:T(8,128)(2,1)S(1)}, bf16[4,2,32,1024]{3,2,1,0:T(8,128)(2,1)}, u32[]{:S(2)}) %copy-start) | copy-done | bytes 524312
  1.0 0.0 copy-start.1
  1.0 1.0 %copy-done.1 = bf16[640,256]{1,0:T(8,128)(2,1)S(1)} copy-done((bf16[640,256]{1,0:T(8,128)(2,1)S(1)}, bf16[640,256]{1,0:T(8,128)(2,1)}, u32[]{:S(2)}) %copy-start.1) | copy-done | bytes 327704
  2.0 0.0 copy-start.2
  2.0 0.9 %copy-done.2 = bf16[256,320]{1,0:T(8,128)(2,1)S(1)} copy-done((bf16[256,320]{1,0:T(8,128)(2,1)S(1)}, bf16[256,320]{1,0:T(8,128)(2,1)}, u32[]{:S(2)}) %copy-start.2) | copy-done | bytes 163864
  2.9 0.0 copy-start.3
  2.9 0.9 %copy-done.3 = bf16[320,256]{1,0:T(8,128)(2,1)S(1)} copy-done((bf16[320,256]{1,0:T(8,128)(2,1)S(1)}, bf16[320,256]{1,0:T(8,128)(2,1)}, u32[]{:S(2)}) %copy-start.3) | copy-done | bytes 163864
  3.9 0.0 copy-start.4
  3.9 0.9 %copy-done.4 = bf16[256,256]{1,0:T(8,128)(2,1)S(1)} copy-done((bf16[256,256]{1,0:T(8,128)(2,1)S(1)}, bf16[256,256]{1,0:T(8,128)(2,1)}, u32[]{:S(2)}) %copy-start.4) | copy-done | bytes 131096
  4.8 0.0 copy-start.5
  4.8 0.9 %copy-done.5 = bf16[192,192]{1,0:T(8,128)(2,1)S(1)} copy-done((bf16[192,192]{1,0:T(8,128)(2,1)S(1)}, bf16[192,192]{1,0:T(8,128)(2,1)}, u32[]{:S(2)}) %copy-start.5) | copy-done | bytes 73752
  5.7 0.0 copy-start.6
  5.7 0.9 %copy-done.6 = bf16[160,256]{1,0:T(8,128)(2,1)S(1)} copy-done((bf16[160,256]{1,0:T(8,128)(2,1)S(1)}, bf16[160,256]{1,0:T(8,128)(2,1)}, u32[]{:S(2)}) %copy-start.6) | copy-done | bytes 81944
  6.5 0.0 copy-start.7
  6.5 0.8 %copy-done.7 = bf16[128,160]{1,0:T(8,128)(2,1)S(1)} copy-done((bf16[128,160]{1,0:T(8,128)(2,1)S(1)}, bf16[128,160]{1,0:T(8,128)(2,1)}, u32[]{:S(2)}) %copy-start.7) | copy-done | bytes 40984
  7.4 0.0 copy-start.8
  7.4 0.8 %copy-done.8 = bf16[256,128]{1,0:T(8,128)(2,1)S(1)} copy-done((bf16[256,128]{1,0:T(8,128)(2,1)S(1)}, bf16[256,128]{1,0:T(8,128)(2,1)}, u32[]{:S(2)}) %copy-start.8) | copy-done | bytes 65560
  8.2 0.0 copy-start.9
  8.2 0.8 %copy-done.9 = bf16[192,64]{1,0:T(8,128)(2,1)S(1)} copy-done((bf16[192,64]{1,0:T(8,128)(2,1)S(1)}, bf16[192,64]{1,0:T(8,128)(2,1)}, u32[]{:S(2)}) %copy-start.9) | copy-done | bytes 24600
  9.0 0.0 copy-start.10
  9.0 0.8 %copy-done.10 = bf16[192,128]{1,0:T(8,128)(2,1)S(1)} copy-done((bf16[192,128]{1,0:T(8,128)(2,1)S(1)}, bf16[192,128]{1,0:T(8,128)(2,1)}, u32[]{:S(2)}) %copy-start.10) | copy-done | bytes 49176
  9.8 32.1 %shard_map.118 = f32[128,4096]{1,0:T(8,128)S(1)} custom-call(f32[128,4096]{1,0:T(8,128)} %image.1, bf16[256,1024]{1,0:T(8,128)(2,1)S(1)} %bitcast.1, bf16[256,128]{1,0:T(8,128)(2,1)S(1)} %copy-done.8, bf16[320,256]{1,0:T(8,128)(2,1)S(1)} %copy-done.3, bf16[640,256]{1,0:T(8,128)(2,1)S(1)} %copy-done.1, bf16[192,128]{1,0:T(8,128)(2,1)S(1)} %copy-done.10, ...), custom_call_target="tpu_custom_call" | custom-call | tf_op jit(solution)/shard_map/pallas_call | solution.py:331
  41.9 1.3 %copy.14 = f32[128,4096]{1,0:T(8,128)} copy(f32[128,4096]{1,0:T(8,128)S(1)} %shard_map.118) | data formatting | bytes 4194304
Async XLA Ops:
  0.0 1.0 %copy-start = (bf16[4,2,32,1024]{3,2,1,0:T(8,128)(2,1)S(1)}, bf16[4,2,32,1024]{3,2,1,0:T(8,128)(2,1)}, u32[]{:S(2)}) copy-start(bf16[4,2,32,1024]{3,2,1,0:T(8,128)(2,1)} %param.13) | copy-start | bytes 1572868
  1.0 1.0 %copy-start.1 = (bf16[640,256]{1,0:T(8,128)(2,1)S(1)}, bf16[640,256]{1,0:T(8,128)(2,1)}, u32[]{:S(2)}) copy-start(bf16[640,256]{1,0:T(8,128)(2,1)} %constant.22.clone.gzp) | copy-start | bytes 983044
  2.0 0.9 %copy-start.2 = (bf16[256,320]{1,0:T(8,128)(2,1)S(1)}, bf16[256,320]{1,0:T(8,128)(2,1)}, u32[]{:S(2)}) copy-start(bf16[256,320]{1,0:T(8,128)(2,1)} %constant.29.clone.phalo) | copy-start | bytes 491524
  2.9 0.9 %copy-start.3 = (bf16[320,256]{1,0:T(8,128)(2,1)S(1)}, bf16[320,256]{1,0:T(8,128)(2,1)}, u32[]{:S(2)}) copy-start(bf16[320,256]{1,0:T(8,128)(2,1)} %constant.21.clone.gz) | copy-start | bytes 491524
  3.9 0.9 %copy-start.4 = (bf16[256,256]{1,0:T(8,128)(2,1)S(1)}, bf16[256,256]{1,0:T(8,128)(2,1)}, u32[]{:S(2)}) copy-start(bf16[256,256]{1,0:T(8,128)(2,1)} %constant.28.clone.pown) | copy-start | bytes 393220
  4.8 0.9 %copy-start.5 = (bf16[192,192]{1,0:T(8,128)(2,1)S(1)}, bf16[192,192]{1,0:T(8,128)(2,1)}, u32[]{:S(2)}) copy-start(bf16[192,192]{1,0:T(8,128)(2,1)} %constant.25.clone.gy) | copy-start | bytes 221188
  5.7 0.9 %copy-start.6 = (bf16[160,256]{1,0:T(8,128)(2,1)S(1)}, bf16[160,256]{1,0:T(8,128)(2,1)}, u32[]{:S(2)}) copy-start(bf16[160,256]{1,0:T(8,128)(2,1)} %constant.27.clone.ix) | copy-start | bytes 245764
  6.5 0.8 %copy-start.7 = (bf16[128,160]{1,0:T(8,128)(2,1)S(1)}, bf16[128,160]{1,0:T(8,128)(2,1)}, u32[]{:S(2)}) copy-start(bf16[128,160]{1,0:T(8,128)(2,1)} %constant.26.clone.iz) | copy-start | bytes 122884
  7.4 0.8 %copy-start.8 = (bf16[256,128]{1,0:T(8,128)(2,1)S(1)}, bf16[256,128]{1,0:T(8,128)(2,1)}, u32[]{:S(2)}) copy-start(bf16[256,128]{1,0:T(8,128)(2,1)} %constant.20.clone.fx) | copy-start | bytes 196612
  8.2 0.8 %copy-start.9 = (bf16[192,64]{1,0:T(8,128)(2,1)S(1)}, bf16[192,64]{1,0:T(8,128)(2,1)}, u32[]{:S(2)}) copy-start(bf16[192,64]{1,0:T(8,128)(2,1)} %constant.24.clone.fyp) | copy-start | bytes 73732
  9.0 0.8 %copy-start.10 = (bf16[192,128]{1,0:T(8,128)(2,1)S(1)}, bf16[192,128]{1,0:T(8,128)(2,1)}, u32[]{:S(2)}) copy-start(bf16[192,128]{1,0:T(8,128)(2,1)} %constant.23.clone.fy) | copy-start | bytes 147460

commit v3 on v2

--- a/solution.py
+++ b/solution.py
@@ -113,11 +113,16 @@
 EDGE = HALF // 4
 
 
-def kernel(image, psfs, fx, gz, gzp, fy, fyp, gy, iz, ix, pown, phalo,
+def kernel(image, psfs, *refs):
+    kernel_body(image, psfs, refs[:10], *refs[10:])
+
+
+def kernel_body(image, psfs, table_refs,
            out,
            img, own, part, halo, d1, e1, spec, pspec, ispec, resp,
            ysend, xsend, yrecv, xrecv, crecv,
-           image_sem, own_sem, psend_sem, precv_sem, rsend_sem, rrecv_sem):
+           fx, gz, gzp, fy, fyp, gy, iz, ix, pown, phalo,
+           image_sem, own_sem, table_sem, psend_sem, precv_sem, rsend_sem, rrecv_sem):
     gx, gy_ = lax.axis_index("gx"), lax.axis_index("gy")
     last_x, last_y = lax.axis_size("gx") - 1, lax.axis_size("gy") - 1
 
@@ -142,6 +147,12 @@
         sl = pl.ds(t * chunk, chunk)
         image_copies.append(pltpu.make_async_copy(image.at[:, sl], img.at[:, sl], image_sem.at[t]))
         image_copies[-1].start()
+
+    order = (fx, gz, gzp, fy, fyp, gy, iz, ix, pown, phalo)
+    table_copies = []
+    for i, (src, dst) in enumerate(zip(table_refs, order)):
+        table_copies.append(pltpu.make_async_copy(src, dst, table_sem.at[i]))
+        table_copies[-1].start()
 
     barrier = pltpu.get_barrier_semaphore()
     count = jnp.int32(0)
@@ -190,6 +201,8 @@
         def _():
             halo[pl.ds(*HALO[side]), :] = jnp.zeros((HALO[side][1], PSFW * PSFW), BF16)
 
+    for copy in table_copies:
+        copy.wait()
     width = 512
     for t in range(INNER // width):
         if t % (chunk // width) == 0:
@@ -331,7 +344,7 @@
     return pl.pallas_call(
         kernel,
         out_shape=jax.ShapeDtypeStruct((TILE, INNER), F32),
-        in_specs=[anywhere, anywhere] + [vmem] * len(consts),
+        in_specs=[anywhere] * (2 + len(consts)),
         out_specs=vmem,
         scratch_shapes=[
             pltpu.VMEM((TILE, INNER), F32),
@@ -349,11 +362,12 @@
             pltpu.VMEM((2, TILE, BAND), BF16),
             pltpu.VMEM((2, HALF, INNER), BF16),
             pltpu.VMEM((4, HALF, BAND), BF16),
-            dma((4,)), dma, dma((8,)), dma((8,)), dma((8,)), dma((8,)),
+            *[pltpu.VMEM(c.shape, BF16) for c in consts],
+            dma((4,)), dma, dma((len(consts),)), dma((8,)), dma((8,)), dma((8,)), dma((8,)),
         ],
         compiler_params=pltpu.CompilerParams(
-            vmem_limit_bytes=49 * 1024 * 1024, collective_id=0, has_side_effects=True),
-    )(image, psfs.reshape(8 * PSFW, PSFW * PSFW), *consts)
+            vmem_limit_bytes=40 * 1024 * 1024, collective_id=0, has_side_effects=True),
+    )(*[pltpu.with_memory_space_constraint(v, pltpu.HBM) for v in (image, psfs.reshape(8 * PSFW, PSFW * PSFW), *consts)])
 
 
 def body(image, psfs):

time: 43.8 us -> 33.7 us (0.77); the launches traced: 43.3 us -> 33.6 us
  local copies, waits for them, and re-layouts: 11.1 us -> 1.32 us
    unnamed x23 -> x1, local copies, waits for them, and re-layouts: 11.1 us -> 1.32 us
where the time goes in v3:
time: 33.7 us; the launch traced here: 33.6 us
  Pallas kernels  32.3 us (96%)
  local copies, waits for them, and re-layouts  1.32 us (4%)
    pallas_call x1, Pallas kernels, compute(): pl.pallas_call(kernel, out_shape=jax.ShapeDtypeStruct((TILE, INNER), F32)...  32.3 us
    unnamed x1, local copies, waits for them, and re-layouts  1.32 us

profile of v3, /device:TPU:166, one launch (start us, length us, event | category | flops | bytes accessed | tf_op | source)
XLA Modules:
  0.0 33.6 jit_solution(16940607684991552927)
XLA Ops:
  0.0 32.3 %shard_map.118 = f32[128,4096]{1,0:T(8,128)S(1)} custom-call(f32[128,4096]{1,0:T(8,128)} %image.1, bf16[256,1024]{1,0:T(8,128)(2,1)} %bitcast.1, bf16[256,128]{1,0:T(8,128)(2,1)} %constant.20.clone.refs_0_, bf16[320,256]{1,0:T(8,128)(2,1)} %constant.21.clone.refs_1_, bf16[640,256]{1,0:T(8,128)(2,1)} %constant.22.clone.refs_2_, ...), custom_call_target="tpu_custom_call" | custom-call | tf_op jit(solution)/shard_map/pallas_call | solution.py:344
  32.3 1.3 %copy.14 = f32[128,4096]{1,0:T(8,128)} copy(f32[128,4096]{1,0:T(8,128)S(1)} %shard_map.118) | data formatting | bytes 4194304

commit v4 on v3

--- a/solution.py
+++ b/solution.py
@@ -120,7 +120,7 @@
 def kernel_body(image, psfs, table_refs,
            out,
            img, own, part, halo, d1, e1, spec, pspec, ispec, resp,
-           ysend, xsend, yrecv, xrecv, crecv,
+           ysend, xsend, esend, yrecv, xrecv, erecv, crecv,
            fx, gz, gzp, fy, fyp, gy, iz, ix, pown, phalo,
            image_sem, own_sem, table_sem, psend_sem, precv_sem, rsend_sem, rrecv_sem):
     gx, gy_ = lax.axis_index("gx"), lax.axis_index("gy")
@@ -141,18 +141,20 @@
 
     own_copy = pltpu.make_async_copy(psfs, own, own_sem)
     own_copy.start()
+    order = (fx, gz, gzp, fy, fyp, gy, iz, ix, pown, phalo)
+    tables_in = {}
+    for i, (src, dst) in enumerate(zip(table_refs, order)):
+        tables_in[i] = pltpu.make_async_copy(src, dst, table_sem.at[i])
     chunk = INNER // 4
     image_copies = []
     for t in range(4):
         sl = pl.ds(t * chunk, chunk)
         image_copies.append(pltpu.make_async_copy(image.at[:, sl], img.at[:, sl], image_sem.at[t]))
-        image_copies[-1].start()
-
-    order = (fx, gz, gzp, fy, fyp, gy, iz, ix, pown, phalo)
-    table_copies = []
-    for i, (src, dst) in enumerate(zip(table_refs, order)):
-        table_copies.append(pltpu.make_async_copy(src, dst, table_sem.at[i]))
-        table_copies[-1].start()
+    tables_in[0].start()
+    for copy in image_copies:
+        copy.start()
+    for i in range(1, len(order)):
+        tables_in[i].start()
 
     barrier = pltpu.get_barrier_semaphore()
     count = jnp.int32(0)
@@ -164,21 +166,6 @@
             pl.semaphore_signal(barrier, inc=1, device_id=place(side), device_id_type=MESH)
 
     own_copy.wait()
-
-    def node(r, c):
-        row = (r * 2 + c) * NODE
-        return own[row:row + NODE, :].astype(F32)
-
-    def put(row, value):
-        part[row:row + NODE, :] = value.astype(BF16)
-
-    w0, w1 = BLEND[0], BLEND[1]
-    for col, at in ((0, 0), (1, 64)):
-        n0, n1, n2, n3 = (node(r, col) for r in range(4))
-        put(at, (w0 * w1) * (n0 + n1) + (w0 * w0) * n2)
-        put(at + NODE, (w0 * w0) * n1 + (w0 * w1) * (n2 + n3))
-    put(128, (w0 * w1) * (node(0, 0) + node(0, 1)))
-    put(160, (w0 * w1) * (node(3, 0) + node(3, 1)))
     corner = {UL: 0, UR: 1, DL: 6, DR: 7}
 
     def psf_copy(side, target=None):
@@ -192,17 +179,36 @@
             device_id=place(side if target is None else target), device_id_type=MESH)
 
     pl.semaphore_wait(barrier, count)
+    for side in range(4, 8):
+        @pl.when(present(side))
+        def _():
+            psf_copy(side).start()
+
+    def node(r, c):
+        row = (r * 2 + c) * NODE
+        return own[row:row + NODE, :].astype(F32)
+
+    def put(row, value):
+        part[row:row + NODE, :] = value.astype(BF16)
+
+    w0, w1 = BLEND[0], BLEND[1]
+    for col, at in ((0, 0), (1, 64)):
+        n0, n1, n2, n3 = (node(r, col) for r in range(4))
+        put(at, (w0 * w1) * (n0 + n1) + (w0 * w0) * n2)
+        put(at + NODE, (w0 * w0) * n1 + (w0 * w1) * (n2 + n3))
+    put(128, (w0 * w1) * (node(0, 0) + node(0, 1)))
+    put(160, (w0 * w1) * (node(3, 0) + node(3, 1)))
     for side in range(8):
-        @pl.when(present(side))
-        def _():
-            psf_copy(side).start()
+        if side < 4:
+            @pl.when(present(side))
+            def _():
+                psf_copy(side).start()
 
         @pl.when(jnp.logical_not(present(side)))
         def _():
             halo[pl.ds(*HALO[side]), :] = jnp.zeros((HALO[side][1], PSFW * PSFW), BF16)
 
-    for copy in table_copies:
-        copy.wait()
+    tables_in[0].wait()
     width = 512
     for t in range(INNER // width):
         if t % (chunk // width) == 0:
@@ -224,6 +230,9 @@
                     block = res[row:row + LZ, jj * LANES:(jj + 1) * LANES]
                     start = part * width_y + (2 * t + jj) * ylo + y
                     out[pl.ds(start, LZ, stride=stride), :] = block
+
+    for i in range(1, len(order)):
+        tables_in[i].wait()
 
     @pl.loop(0, 16, unroll=U_DEPTH)
     def _(t):
@@ -278,28 +287,39 @@
             cols = pl.ds(pl.multiple_of(e * 256, 256), 256)
             ysend[side, :, cols] = group(e + side * (GROUPS - EDGE)).astype(BF16)
 
-    def y_copy(side, target):
-        dx, dy = SIDES[side]
-        rows = {0: pl.ds(HALF, TILE), -1: pl.ds(0, HALF), 1: pl.ds(HALF + TILE, HALF)}[dx]
-        dst = yrecv.at[BACK[side]] if dx == 0 else crecv.at[BACK[side] - 4]
+    def remote(src, dst, send_sem, recv_sem, at, side, target):
         return pltpu.make_async_remote_copy(
-            src_ref=ysend.at[side if dx == 0 else (dy + 1) // 2, rows, :], dst_ref=dst,
-            send_sem=rsend_sem.at[side], recv_sem=rrecv_sem.at[BACK[side]],
+            src_ref=src, dst_ref=dst, send_sem=send_sem.at[at + side], recv_sem=recv_sem.at[at + BACK[side]],
             device_id=place(side if target is None else target), device_id_type=MESH)
 
-    def x_copy(side, target):
-        return pltpu.make_async_remote_copy(
-            src_ref=xsend.at[side - 2], dst_ref=xrecv.at[BACK[side] - 2],
-            send_sem=rsend_sem.at[side], recv_sem=rrecv_sem.at[BACK[side]],
-            device_id=place(side if target is None else target), device_id_type=MESH)
-
-    def response_copy(side, target=None):
-        return (x_copy if side in (UP, DOWN) else y_copy)(side, target)
-
-    for side in (LEFT, RIGHT, UL, UR, DL, DR):
-        @pl.when(present(side))
-        def _():
-            response_copy(side).start()
+    mid = TILE - 2 * HALF
+    inner = pl.ds(2 * HALF, mid)
+
+    def mid_copy(side, target=None):
+        return remote(ysend.at[side, inner, :], yrecv.at[BACK[side]], rsend_sem, rrecv_sem, 0, side, target)
+
+    def corner_copy(side, target=None):
+        rows = pl.ds(0 if side == UP else HALF + TILE, HALF)
+        return remote(ysend.at[:, rows, :], crecv.at[BACK[side] - 2], rsend_sem, rrecv_sem, 0, side, target)
+
+    def edge_copy(side, target=None):
+        return remote(esend.at[side], erecv.at[BACK[side]], rsend_sem, rrecv_sem, 4, side, target)
+
+    def band_copy(side, target=None):
+        return remote(xsend.at[side - 2], xrecv.at[BACK[side] - 2], rsend_sem, rrecv_sem, 4, side, target)
+
+    first_copy = (mid_copy, mid_copy, corner_copy, corner_copy)
+    second_copy = (edge_copy, edge_copy, band_copy, band_copy)
+
+    for side in (UP, DOWN, LEFT, RIGHT):
+        @pl.when(present(side))
+        def _():
+            first_copy[side](side).start()
+
+    for side in (UP, DOWN):
+        @pl.when(jnp.logical_not(present(side)))
+        def _():
+            crecv[side - 2] = jnp.zeros((2, HALF, BAND), BF16)
 
     @pl.loop(0, GROUPS - 2 * EDGE, unroll=U_INNER)
     def _(g):
@@ -312,30 +332,49 @@
     for side in (UP, DOWN):
         @pl.when(present(side))
         def _():
-            response_copy(side).start()
-
-    def arrive(side, rows, cols, ref):
-        @pl.when(present(side))
-        def _():
-            response_copy(BACK[side], side).wait_recv()
-            out[rows, cols] += ref[...].astype(F32)
+            band_copy(side).start()
+
+    for side in (UP, DOWN):
+        @pl.when(present(side))
+        def _():
+            corner_copy(BACK[side], side).wait_recv()
+
+    for side in (LEFT, RIGHT):
+        for end in range(2):
+            rows = slice(HALF + end * (TILE - HALF), 2 * HALF + end * (TILE - HALF))
+            esend[side, end] = (ysend[side, rows, :].astype(F32) + crecv[end, side].astype(F32)).astype(BF16)
+
+        @pl.when(present(side))
+        def _():
+            edge_copy(side).start()
 
     top, bottom = pl.ds(0, HALF), pl.ds(TILE - HALF, HALF)
-    first, last = pl.ds(0, BAND), pl.ds(INNER - BAND, BAND)
-    every = pl.ds(0, TILE)
-    arrive(UP, top, pl.ds(0, INNER), xrecv.at[0])
-    arrive(DOWN, bottom, pl.ds(0, INNER), xrecv.at[1])
-    arrive(UL, top, first, crecv.at[0])
-    arrive(DL, bottom, first, crecv.at[2])
-    arrive(LEFT, every, first, yrecv.at[0])
-    arrive(UR, top, last, crecv.at[1])
-    arrive(DR, bottom, last, crecv.at[3])
-    arrive(RIGHT, every, last, yrecv.at[1])
+    columns = (pl.ds(0, BAND), pl.ds(INNER - BAND, BAND))
+    for side, rows in ((UP, top), (DOWN, bottom)):
+        @pl.when(present(side))
+        def _():
+            band_copy(BACK[side], side).wait_recv()
+            out[rows, :] += xrecv[side - 2].astype(F32)
+
+    for side in (LEFT, RIGHT):
+        @pl.when(present(side))
+        def _():
+            mid_copy(BACK[side], side).wait_recv()
+            out[pl.ds(HALF, mid), columns[side]] += yrecv[side].astype(F32)
+            edge_copy(BACK[side], side).wait_recv()
+            out[top, columns[side]] += erecv[side, 0].astype(F32)
+            out[bottom, columns[side]] += erecv[side, 1].astype(F32)
+
     for side in range(8):
         @pl.when(present(side))
         def _():
             psf_copy(side).wait_send()
-            response_copy(side).wait_send()
+
+    for side in range(4):
+        @pl.when(present(side))
+        def _():
+            first_copy[side](side).wait_send()
+            second_copy[side](side).wait_send()
 
 
 def compute(image, psfs, *consts):
@@ -359,9 +398,11 @@
             pltpu.VMEM((LXY * SZ, LANES), F32),
             pltpu.VMEM((2, EXT, BAND), BF16),
             pltpu.VMEM((2, HALF, INNER), BF16),
-            pltpu.VMEM((2, TILE, BAND), BF16),
+            pltpu.VMEM((2, 2, HALF, BAND), BF16),
+            pltpu.VMEM((2, TILE - 2 * HALF, BAND), BF16),
             pltpu.VMEM((2, HALF, INNER), BF16),
-            pltpu.VMEM((4, HALF, BAND), BF16),
+            pltpu.VMEM((2, 2, HALF, BAND), BF16),
+            pltpu.VMEM((2, 2, HALF, BAND), BF16),
             *[pltpu.VMEM(c.shape, BF16) for c in consts],
             dma((4,)), dma, dma((len(consts),)), dma((8,)), dma((8,)), dma((8,)), dma((8,)),
         ],

time: 33.7 us -> 32.1 us (0.953)
  the two profiles are of different devices: /device:TPU:166 before, /device:TPU:5 now
where the time goes in v4:
time: 32.1 us; the launch traced here: 32 us
  Pallas kernels  30.7 us (96%)
  local copies, waits for them, and re-layouts  1.32 us (4%)
    pallas_call x1, Pallas kernels, compute(): pl.pallas_call(kernel, out_shape=jax.ShapeDtypeStruct((TILE, INNER), F32)...  30.7 us
    unnamed x1, local copies, waits for them, and re-layouts  1.32 us

profile of v4, /device:TPU:5, one launch (start us, length us, event | category | flops | bytes accessed | tf_op | source)
XLA Modules:
  0.0 32.0 jit_solution(6369115981361533990)
XLA Ops:
  0.0 30.7 %shard_map.118 = f32[128,4096]{1,0:T(8,128)S(1)} custom-call(f32[128,4096]{1,0:T(8,128)} %image.1, bf16[256,1024]{1,0:T(8,128)(2,1)} %bitcast.1, bf16[256,128]{1,0:T(8,128)(2,1)} %constant.20.clone.refs_0_, bf16[320,256]{1,0:T(8,128)(2,1)} %constant.21.clone.refs_1_, bf16[640,256]{1,0:T(8,128)(2,1)} %constant.22.clone.refs_2_, ...), custom_call_target="tpu_custom_call" | custom-call | tf_op jit(solution)/shard_map/pallas_call | solution.py:383
  30.7 1.3 %copy.14 = f32[128,4096]{1,0:T(8,128)} copy(f32[128,4096]{1,0:T(8,128)S(1)} %shard_map.118) | data formatting | bytes 4194304

commit v5 on v4

--- a/solution.py
+++ b/solution.py
@@ -311,7 +311,7 @@
     first_copy = (mid_copy, mid_copy, corner_copy, corner_copy)
     second_copy = (edge_copy, edge_copy, band_copy, band_copy)
 
-    for side in (UP, DOWN, LEFT, RIGHT):
+    for side in (UP, DOWN):
         @pl.when(present(side))
         def _():
             first_copy[side](side).start()
@@ -333,6 +333,11 @@
         @pl.when(present(side))
         def _():
             band_copy(side).start()
+
+    for side in (LEFT, RIGHT):
+        @pl.when(present(side))
+        def _():
+            mid_copy(side).start()
 
     for side in (UP, DOWN):
         @pl.when(present(side))

time: 32.1 us -> 31.5 us (0.981)
  the two profiles are of different devices: /device:TPU:5 before, /device:TPU:165 now
where the time goes in v5:
time: 31.5 us
  Pallas kernels  30.1 us (96%)
  local copies, waits for them, and re-layouts  1.32 us (4%)
    pallas_call x1, Pallas kernels, compute(): pl.pallas_call(kernel, out_shape=jax.ShapeDtypeStruct((TILE, INNER), F32)...  30.1 us
    unnamed x1, local copies, waits for them, and re-layouts  1.32 us

profile of v5, /device:TPU:165, one launch (start us, length us, event | category | flops | bytes accessed | tf_op | source)
XLA Modules:
  0.0 31.5 jit_solution(8528951602320216673)
XLA Ops:
  0.0 30.1 %shard_map.118 = f32[128,4096]{1,0:T(8,128)S(1)} custom-call(f32[128,4096]{1,0:T(8,128)} %image.1, bf16[256,1024]{1,0:T(8,128)(2,1)} %bitcast.1, bf16[256,128]{1,0:T(8,128)(2,1)} %constant.20.clone.refs_0_, bf16[320,256]{1,0:T(8,128)(2,1)} %constant.21.clone.refs_1_, bf16[640,256]{1,0:T(8,128)(2,1)} %constant.22.clone.refs_2_, ...), custom_call_target="tpu_custom_call" | custom-call | tf_op jit(solution)/shard_map/pallas_call | solution.py:388
  30.1 1.3 %copy.14 = f32[128,4096]{1,0:T(8,128)} copy(f32[128,4096]{1,0:T(8,128)S(1)} %shard_map.118) | data formatting | bytes 4194304

commit v6 on v3

--- a/solution.py
+++ b/solution.py
@@ -141,18 +141,20 @@
 
     own_copy = pltpu.make_async_copy(psfs, own, own_sem)
     own_copy.start()
+    order = (fx, gz, gzp, fy, fyp, gy, iz, ix, pown, phalo)
+    tables_in = {}
+    for i, (src, dst) in enumerate(zip(table_refs, order)):
+        tables_in[i] = pltpu.make_async_copy(src, dst, table_sem.at[i])
     chunk = INNER // 4
     image_copies = []
     for t in range(4):
         sl = pl.ds(t * chunk, chunk)
         image_copies.append(pltpu.make_async_copy(image.at[:, sl], img.at[:, sl], image_sem.at[t]))
-        image_copies[-1].start()
-
-    order = (fx, gz, gzp, fy, fyp, gy, iz, ix, pown, phalo)
-    table_copies = []
-    for i, (src, dst) in enumerate(zip(table_refs, order)):
-        table_copies.append(pltpu.make_async_copy(src, dst, table_sem.at[i]))
-        table_copies[-1].start()
+    tables_in[0].start()
+    for copy in image_copies:
+        copy.start()
+    for i in range(1, len(order)):
+        tables_in[i].start()
 
     barrier = pltpu.get_barrier_semaphore()
     count = jnp.int32(0)
@@ -164,21 +166,6 @@
             pl.semaphore_signal(barrier, inc=1, device_id=place(side), device_id_type=MESH)
 
     own_copy.wait()
-
-    def node(r, c):
-        row = (r * 2 + c) * NODE
-        return own[row:row + NODE, :].astype(F32)
-
-    def put(row, value):
-        part[row:row + NODE, :] = value.astype(BF16)
-
-    w0, w1 = BLEND[0], BLEND[1]
-    for col, at in ((0, 0), (1, 64)):
-        n0, n1, n2, n3 = (node(r, col) for r in range(4))
-        put(at, (w0 * w1) * (n0 + n1) + (w0 * w0) * n2)
-        put(at + NODE, (w0 * w0) * n1 + (w0 * w1) * (n2 + n3))
-    put(128, (w0 * w1) * (node(0, 0) + node(0, 1)))
-    put(160, (w0 * w1) * (node(3, 0) + node(3, 1)))
     corner = {UL: 0, UR: 1, DL: 6, DR: 7}
 
     def psf_copy(side, target=None):
@@ -191,18 +178,37 @@
             send_sem=psend_sem.at[side], recv_sem=precv_sem.at[BACK[side]],
             device_id=place(side if target is None else target), device_id_type=MESH)
 
+    def node(r, c):
+        row = (r * 2 + c) * NODE
+        return own[row:row + NODE, :].astype(F32)
+
+    def put(row, value):
+        part[row:row + NODE, :] = value.astype(BF16)
+
+    w0, w1 = BLEND[0], BLEND[1]
+    put(128, (w0 * w1) * (node(0, 0) + node(0, 1)))
+    put(160, (w0 * w1) * (node(3, 0) + node(3, 1)))
     pl.semaphore_wait(barrier, count)
+    for side in range(2, 8):
+        @pl.when(present(side))
+        def _():
+            psf_copy(side).start()
+
+    for side in (LEFT, RIGHT):
+        n0, n1, n2, n3 = (node(r, side) for r in range(4))
+        put(side * 64, (w0 * w1) * (n0 + n1) + (w0 * w0) * n2)
+        put(side * 64 + NODE, (w0 * w0) * n1 + (w0 * w1) * (n2 + n3))
+
+        @pl.when(present(side))
+        def _():
+            psf_copy(side).start()
+
     for side in range(8):
-        @pl.when(present(side))
-        def _():
-            psf_copy(side).start()
-
         @pl.when(jnp.logical_not(present(side)))
         def _():
             halo[pl.ds(*HALO[side]), :] = jnp.zeros((HALO[side][1], PSFW * PSFW), BF16)
 
-    for copy in table_copies:
-        copy.wait()
+    tables_in[0].wait()
     width = 512
     for t in range(INNER // width):
         if t % (chunk // width) == 0:
@@ -224,6 +230,9 @@
                     block = res[row:row + LZ, jj * LANES:(jj + 1) * LANES]
                     start = part * width_y + (2 * t + jj) * ylo + y
                     out[pl.ds(start, LZ, stride=stride), :] = block
+
+    for i in range(1, len(order)):
+        tables_in[i].wait()
 
     @pl.loop(0, 16, unroll=U_DEPTH)
     def _(t):
@@ -296,7 +305,7 @@
     def response_copy(side, target=None):
         return (x_copy if side in (UP, DOWN) else y_copy)(side, target)
 
-    for side in (LEFT, RIGHT, UL, UR, DL, DR):
+    for side in (UL, UR, DL, DR):
         @pl.when(present(side))
         def _():
             response_copy(side).start()
@@ -309,7 +318,7 @@
         xsend[0, :, cols] = value[:HALF].astype(BF16)
         xsend[1, :, cols] = value[HALF + TILE:].astype(BF16)
 
-    for side in (UP, DOWN):
+    for side in (UP, DOWN, LEFT, RIGHT):
         @pl.when(present(side))
         def _():
             response_copy(side).start()

time: 33.7 us -> 31.2 us (0.926); the launches traced: 33.6 us -> 30.7 us
  Pallas kernels: 32.3 us -> 29.4 us
    pallas_call x1, Pallas kernels: 32.3 us -> 29.4 us  [compute(): pl.pallas_call(kernel, out_shape=jax.ShapeDtypeStruct((TILE, INNER), F32)...]
where the time goes in v6:
time: 31.2 us; the launch traced here: 30.7 us
  Pallas kernels  29.4 us (94%)
  local copies, waits for them, and re-layouts  1.32 us (4%)
    pallas_call x1, Pallas kernels, compute(): pl.pallas_call(kernel, out_shape=jax.ShapeDtypeStruct((TILE, INNER), F32)...  29.4 us
    unnamed x1, local copies, waits for them, and re-layouts  1.32 us

profile of v6, /device:TPU:166, one launch (start us, length us, event | category | flops | bytes accessed | tf_op | source)
XLA Modules:
  0.0 30.7 jit_solution(2455681909604765571)
XLA Ops:
  0.0 29.4 %shard_map.118 = f32[128,4096]{1,0:T(8,128)S(1)} custom-call(f32[128,4096]{1,0:T(8,128)} %image.1, bf16[256,1024]{1,0:T(8,128)(2,1)} %bitcast.1, bf16[256,128]{1,0:T(8,128)(2,1)} %constant.20.clone.refs_0_, bf16[320,256]{1,0:T(8,128)(2,1)} %constant.21.clone.refs_1_, bf16[640,256]{1,0:T(8,128)(2,1)} %constant.22.clone.refs_2_, ...), custom_call_target="tpu_custom_call" | custom-call | tf_op jit(solution)/shard_map/pallas_call | solution.py:353
  29.4 1.3 %copy.14 = f32[128,4096]{1,0:T(8,128)} copy(f32[128,4096]{1,0:T(8,128)S(1)} %shard_map.118) | data formatting | bytes 4194304
